TPU v7x, 1024 devices: a whole 8x8x8 slice. The times are simulated.
1024 devices in a mesh: seq: 16 (over x, core), chan: 64 (over y, z).
Axes of the slice: x: 8, y: 8, z: 8, core: 2. Of those that a mesh axis runs over, the one named last changes fastest.
Arguments:
- tokens: bfloat16 [2048, 8192], P('seq', 'chan'), may hold values from -6 to 6
- in_weight: bfloat16 [8192, 3, 8192], P(None, None, 'chan'), may hold values from -0.0625 to 0.0625
- long_filter: float32 [2048, 8192], P('seq', 'chan'), may hold values from -1 to 1
- grad_out: bfloat16 [2048, 8192], P('seq', 'chan'), may hold values from -6 to 6
Outputs:
- gated_out: bfloat16 [2048, 8192], P('seq', 'chan')
- grad_proj: bfloat16 [2048, 3, 8192], P('seq', None, 'chan')
- grad_filter: float32 [2048, 8192], P('seq', 'chan')
All inputs are finite; a program needn't handle non-finite values.
Results may differ from a plain program's by a relative error of at most 0.0064.
Values may be sent and summed in bfloat16 or wider, within the bound.
A program may use at most 64 MiB of HBM per device.

v0:
```python
import math

import jax
import jax.numpy as jnp
from jax import lax
from jax.sharding import PartitionSpec as P


def from_partner(value, axis, stride):
    mask = 2**stride
    pairs = [(source, source ^ mask) for source in range(lax.axis_size(axis))]
    return lax.ppermute(value, axis, pairs)


def bit_reverse(number, bit_count):
    result = number * 0
    for bit_pos in range(bit_count):
        result = result + number // 2**bit_pos % 2 * 2 ** (bit_count - 1 - bit_pos)
    return result


def rotate(state, angle):
    cosine = jnp.cos(angle)
    sine = jnp.sin(angle)
    real_part = state[:, 0]
    imag_part = state[:, 1]
    return jnp.stack(
        [real_part * cosine - imag_part * sine, real_part * sine + imag_part * cosine], axis=1
    )


def pair_swap(state, bit_pos):
    return from_partner(state, "seq", bit_pos)


def across_blocks(state, inverse, seq_index, bit_count):
    if inverse:
        for bit_pos in range(bit_count):
            half_span = 2**bit_pos
            partner = pair_swap(state, bit_pos)
            upper = (seq_index // half_span % 2).astype(jnp.float32)
            lower = 1.0 - upper
            turn_angle = (
                2.0 * math.pi * (seq_index % half_span).astype(jnp.float32) / (2 * half_span)
            )
            first = lower * state + upper * partner
            second = lower * partner + upper * state
            state = 0.5 * (first + (1.0 - 2.0 * upper) * rotate(second, turn_angle))
    else:
        for bit_pos in range(bit_count - 1, -1, -1):
            half_span = 2**bit_pos
            partner = pair_swap(state, bit_pos)
            upper = (seq_index // half_span % 2).astype(jnp.float32)
            turn_angle = (
                -2.0 * math.pi * (seq_index % half_span).astype(jnp.float32) / (2 * half_span)
            )
            state = rotate(partner + (1.0 - 2.0 * upper) * state, upper * turn_angle)
    return state


def per_device(tokens, in_weight, long_filter, grad_out):
    tok_rows, chan_width = long_filter.shape
    groups = lax.axis_size("seq")
    seq_index = lax.axis_index("seq")
    bit_count = groups.bit_length() - 1
    fft_length = 2 * tok_rows * groups
    w_flat = in_weight.reshape(in_weight.shape[0], 3 * chan_width)
    gathered = lax.all_gather(tokens, "chan", axis=1, tiled=True)
    projected = jnp.dot(gathered, w_flat, preferred_element_type=jnp.float32)
    projection = projected.astype(jnp.bfloat16).reshape(tok_rows, 3, chan_width)
    gate_in = projection[:, 0].astype(jnp.float32)
    gate_out = projection[:, 1].astype(jnp.float32)
    values = projection[:, 2].astype(jnp.float32)
    grad_dense = grad_out.astype(jnp.float32)
    signal = jnp.stack([gate_in * values, long_filter, grad_dense * gate_out], axis=1)
    twist_angle = -math.pi * seq_index.astype(jnp.float32) / groups
    real_half = jnp.stack([signal, signal * jnp.cos(twist_angle)], axis=1)
    imag_half = jnp.stack([jnp.zeros_like(signal), signal * jnp.sin(twist_angle)], axis=1)
    twisted = jnp.stack([real_half, imag_half], axis=1)
    mixed = across_blocks(twisted, False, seq_index, bit_count)
    block_freq = 2 * bit_reverse(seq_index, bit_count) + jnp.arange(2, dtype=jnp.int32)
    row_index = jnp.arange(tok_rows, dtype=jnp.int32)
    frequency = block_freq[:, None, None] + 2 * groups * row_index[None, :, None]
    phase = frequency * row_index[None, None, :] % fft_length
    local_angle = -2.0 * math.pi * phase.astype(jnp.float32) / fft_length
    table_re = jnp.cos(local_angle)
    table_im = jnp.sin(local_angle)
    forward_table = jnp.stack(
        [jnp.stack([table_re, -table_im], axis=2), jnp.stack([table_im, table_re], axis=2)], axis=1
    )
    turned_re = jnp.transpose(table_re, (0, 2, 1))
    turned_im = jnp.transpose(table_im, (0, 2, 1))
    inverse_table = jnp.stack(
        [jnp.stack([turned_re, turned_im], axis=2), jnp.stack([-turned_im, turned_re], axis=2)],
        axis=1,
    )
    spectrum = jnp.einsum(
        "eakbn,nbesc->kaesc", forward_table, mixed, precision=lax.Precision.HIGHEST
    )
    spec_re = spectrum[:, 0]
    spec_im = spectrum[:, 1]
    src_re, src_im = (spec_re[:, :, 0], spec_im[:, :, 0])
    filt_re, filt_im = (spec_re[:, :, 1], spec_im[:, :, 1])
    grad_re, grad_im = (spec_re[:, :, 2], spec_im[:, :, 2])
    prod_re = jnp.stack(
        [
            src_re * filt_re - src_im * filt_im,
            filt_re * grad_re + filt_im * grad_im,
            src_re * grad_re + src_im * grad_im,
        ],
        axis=2,
    )
    prod_im = jnp.stack(
        [
            src_re * filt_im + src_im * filt_re,
            filt_re * grad_im - filt_im * grad_re,
            src_re * grad_im - src_im * grad_re,
        ],
        axis=2,
    )
    products = jnp.stack([prod_re, prod_im], axis=1)
    back = (
        jnp.einsum("eanbk,kbesc->naesc", inverse_table, products, precision=lax.Precision.HIGHEST)
        / tok_rows
    )
    returned = across_blocks(back, True, seq_index, bit_count)
    final_angle = math.pi * seq_index.astype(jnp.float32) / groups
    combined = 0.5 * (
        returned[:, 0, 0]
        + returned[:, 0, 1] * jnp.cos(final_angle)
        - returned[:, 1, 1] * jnp.sin(final_angle)
    )
    conv_out = combined[:, 0]
    grad_source = combined[:, 1]
    grad_filter = combined[:, 2]
    gated_out = (gate_out * conv_out).astype(jnp.bfloat16)
    grad_proj = jnp.stack(
        [grad_source * values, grad_dense * conv_out, grad_source * gate_in], axis=1
    ).astype(jnp.bfloat16)
    return (gated_out, grad_proj, grad_filter)


def solution(mesh):
    in_specs = (P("seq", "chan"), P(None, None, "chan"), P("seq", "chan"), P("seq", "chan"))
    out_specs = (P("seq", "chan"), P("seq", None, "chan"), P("seq", "chan"))
    return jax.shard_map(
        per_device, mesh=mesh, in_specs=in_specs, out_specs=out_specs, check_vma=False
    )
```

profile of v0, /device:TPU:1, one launch (start us, length us, event | category | flops | bytes accessed | tf_op | source)
XLA Modules:
  0.0 339.6 jit_solution(2997940554973140537)
XLA Ops:
  7.2 0.7 all-gather.2.cloned.1.call-update
  8.1 8.8 %copy.28 = bf16[8192,3,128]{0,2,1:T(8,128)(2,1)} copy(bf16[8192,3,128]{2,0,1:T(8,128)(2,1)} %param.5) | data formatting | bytes 12582912 | tf_op args[1]
  16.8 0.1 copy.31
  17.0 0.1 copy.30
  17.1 94.1 %all-gather.2.cloned.1.call-done = bf16[128,8192]{1,0:T(8,128)(2,1)} async-done(((bf16[128,128]{1,0:T(8,128)(2,1)}), bf16[128,8192]{1,0:T(8,128)(2,1)}) %all-gather.2.cloned.1.call-update) | async-done | bytes 2097168 | tf_op jit(solution)/shard_map/all_gather | solution.py:68
  111.2 5.4 %convolution_convert_fusion = bf16[128,384]{1,0:T(8,128)(2,1)S(1)} fusion(bf16[128,8192]{1,0:T(8,128)(2,1)} %all-gather.2.cloned.1.call-done, bf16[8192,384]{0,1:T(8,128)(2,1)} %bitcast.100), kind=kOutput, calls=%fused_computation.2 | convolution fusion | flops 805355520 | bytes 8486912 | tf_op jit(solution)/shard_map/dot_general | solution.py:69
  116.6 0.1 copy.29
  116.9 7.0 %collective-permute-start = (f32[128,2,2,3,128]{0,4,1,3,2:T(8,128)S(1)}, f32[128,2,2,3,128]{0,4,1,3,2:T(8,128)S(1)}, u32[]{:S(2)}, u32[]{:S(2)}) collective-permute-start(f32[128,2,2,3,128]{0,4,1,3,2:T(8,128)S(1)} %pad_maximum_fusion), channel_id=1, source_target_pairs={{0,512},{64,576},{128,640},{192,704},{256,768},{320,832},{384,896}... | collective-permute-start | bytes 2359304 | tf_op jit(solution)/shard_map/ppermute | solution.py:12
  124.2 23.0 %collective-permute-done = f32[128,2,2,3,128]{0,4,1,3,2:T(8,128)S(1)} collective-permute-done((f32[128,2,2,3,128]{0,4,1,3,2:T(8,128)S(1)}, f32[128,2,2,3,128]{0,4,1,3,2:T(8,128)S(1)}, u32[]{:S(2)}, u32[]{:S(2)}) %collective-permute-start) | collective-permute-done | bytes 786464 | tf_op jit(solution)/shard_map/ppermute | solution.py:12
  147.2 0.1 multiply_add_fusion.6
  147.3 0.1 multiply_subtract_fusion.7
  147.4 14.3 %collective-permute-start.1 = (f32[128,2,2,3,128]{0,4,1,3,2:T(8,128)S(1)}, f32[128,2,2,3,128]{0,4,1,3,2:T(8,128)S(1)}, u32[]{:S(2)}, u32[]{:S(2)}) collective-permute-start(f32[128,2,2,3,128]{0,4,1,3,2:T(8,128)S(1)} %pad_maximum_fusion.1), channel_id=1, source_target_pairs={{0,256},{64,320},{128,384},{192,448},{256,0},{320,64},{384,128},{4... | collective-permute-start | bytes 2359304 | tf_op jit(solution)/shard_map/ppermute | solution.py:12
  162.0 33.8 %collective-permute-done.1 = f32[128,2,2,3,128]{0,4,1,3,2:T(8,128)S(1)} collective-permute-done((f32[128,2,2,3,128]{0,4,1,3,2:T(8,128)S(1)}, f32[128,2,2,3,128]{0,4,1,3,2:T(8,128)S(1)}, u32[]{:S(2)}, u32[]{:S(2)}) %collective-permute-start.1) | collective-permute-done | bytes 786464 | tf_op jit(solution)/shard_map/ppermute | solution.py:12
  195.8 0.1 multiply_add_fusion.5
  195.8 0.1 multiply_subtract_fusion.6
  196.0 1.9 collective-permute-start.2
  198.3 17.3 %collective-permute-done.2 = f32[128,2,2,3,128]{0,4,1,3,2:T(8,128)S(1)} collective-permute-done((f32[128,2,2,3,128]{0,4,1,3,2:T(8,128)S(1)}, f32[128,2,2,3,128]{0,4,1,3,2:T(8,128)S(1)}, u32[]{:S(2)}, u32[]{:S(2)}) %collective-permute-start.2) | collective-permute-done | bytes 786464 | tf_op jit(solution)/shard_map/ppermute | solution.py:12
  215.6 0.1 multiply_add_fusion.4
  215.7 0.1 multiply_subtract_fusion.5
  215.8 4.2 %collective-permute-start.3 = (f32[128,2,2,3,128]{0,4,1,3,2:T(8,128)S(1)}, f32[128,2,2,3,128]{0,4,1,3,2:T(8,128)S(1)}, u32[]{:S(2)}, u32[]{:S(2)}) collective-permute-start(f32[128,2,2,3,128]{0,4,1,3,2:T(8,128)S(1)} %pad_maximum_fusion.3), channel_id=1, source_target_pairs={{0,64},{64,0},{128,192},{192,128},{256,320},{320,256},{384,448},{4... | collective-permute-start | bytes 2359304 | tf_op jit(solution)/shard_map/ppermute | solution.py:12
  220.1 1.1 fusion.35
  221.3 0.6 collective-permute-done.3
  221.9 0.1 multiply_add_fusion.3
  222.0 0.1 multiply_subtract_fusion.4
  222.1 0.9 convolution_bitcast_fusion.1
  223.2 0.9 convolution_bitcast_fusion
  224.2 2.3 collective-permute-start.4
  226.5 1.9 collective-permute-done.4
  228.4 0.1 bitcast_add_fusion
  228.6 0.2 broadcast_multiply_fusion.2
  228.8 1.9 collective-permute-start.5
  230.9 18.6 %collective-permute-done.5 = f32[128,2,2,3,128]{0,4,3,2,1:T(8,128)S(1)} collective-permute-done((f32[128,2,2,3,128]{0,4,3,2,1:T(8,128)S(1)}, f32[128,2,2,3,128]{0,4,3,2,1:T(8,128)S(1)}, u32[]{:S(2)}, u32[]{:S(2)}) %collective-permute-start.5) | collective-permute-done | bytes 786464 | tf_op jit(solution)/shard_map/ppermute | solution.py:12
  249.4 0.1 multiply_add_fusion.2
  249.5 0.1 multiply_subtract_fusion.2
  249.6 0.2 broadcast_multiply_fusion.1
  249.8 1.9 collective-permute-start.6
  251.9 36.7 %collective-permute-done.6 = f32[128,2,2,3,128]{0,4,3,2,1:T(8,128)S(1)} collective-permute-done((f32[128,2,2,3,128]{0,4,3,2,1:T(8,128)S(1)}, f32[128,2,2,3,128]{0,4,3,2,1:T(8,128)S(1)}, u32[]{:S(2)}, u32[]{:S(2)}) %collective-permute-start.6) | collective-permute-done | bytes 786464 | tf_op jit(solution)/shard_map/ppermute | solution.py:12
  288.7 0.1 multiply_add_fusion.1
  288.8 0.1 multiply_subtract_fusion.1
  288.9 0.2 broadcast_multiply_fusion
  289.1 3.9 %collective-permute-start.7 = (f32[128,2,2,3,128]{0,4,3,2,1:T(8,128)S(1)}, f32[128,2,2,3,128]{0,4,3,2,1:T(8,128)S(1)}, u32[]{:S(2)}, u32[]{:S(2)}) collective-permute-start(f32[128,2,2,3,128]{0,4,3,2,1:T(8,128)S(1)} %get-tuple-element.9), channel_id=1, source_target_pairs={{0,512},{64,576},{128,640},{192,704},{256,768},{320,832},{384,896}... | collective-permute-start | bytes 2359304 | tf_op jit(solution)/shard_map/ppermute | solution.py:12
  293.3 36.8 %collective-permute-done.7 = f32[128,2,2,3,128]{0,4,3,2,1:T(8,128)S(1)} collective-permute-done((f32[128,2,2,3,128]{0,4,3,2,1:T(8,128)S(1)}, f32[128,2,2,3,128]{0,4,3,2,1:T(8,128)S(1)}, u32[]{:S(2)}, u32[]{:S(2)}) %collective-permute-start.7) | collective-permute-done | bytes 786464 | tf_op jit(solution)/shard_map/ppermute | solution.py:12
  330.1 0.1 multiply_add_fusion
  330.2 0.1 multiply_subtract_fusion
  330.3 0.2 fusion.6
  330.6 0.8 copy.46
  331.3 0.7 copy.47
  332.1 0.7 copy.45
  (30 shorter events, 1.0 us)
Async XLA Ops:
  7.2 104.0 %all-gather.2.cloned.1.call-start = ((), (), s32[]{:S(2)}) async-start(), calls=%async_computation | async-start | bytes 2129920 | tf_op jit(solution)/shard_map/all_gather | solution.py:68
  8.1 8.8 %copy-start.1 = (bf16[128,128]{1,0:T(8,128)(2,1)S(1)}, bf16[128,128]{1,0:T(8,128)(2,1)}, u32[]{:S(2)}) copy-start(bf16[128,128]{1,0:T(8,128)(2,1)} %param.7) | copy-start | bytes 98308
  8.1 8.9 %copy-start = (f32[128,128]{1,0:T(8,128)S(1)}, f32[128,128]{1,0:T(8,128)}, u32[]{:S(2)}) copy-start(f32[128,128]{1,0:T(8,128)} %param.6) | copy-start | bytes 196612
  116.9 30.2 %collective-permute-start = (f32[128,2,2,3,128]{0,4,1,3,2:T(8,128)S(1)}, f32[128,2,2,3,128]{0,4,1,3,2:T(8,128)S(1)}, u32[]{:S(2)}, u32[]{:S(2)}) collective-permute-start(f32[128,2,2,3,128]{0,4,1,3,2:T(8,128)S(1)} %pad_maximum_fusion), channel_id=1, source_target_pairs={{0,512},{64,576},{128,640},{192,704},{256,768},{320,832},{384,896}... | collective-permute-start | bytes 2359304 | tf_op jit(solution)/shard_map/ppermute | solution.py:12
  147.4 48.3 %collective-permute-start.1 = (f32[128,2,2,3,128]{0,4,1,3,2:T(8,128)S(1)}, f32[128,2,2,3,128]{0,4,1,3,2:T(8,128)S(1)}, u32[]{:S(2)}, u32[]{:S(2)}) collective-permute-start(f32[128,2,2,3,128]{0,4,1,3,2:T(8,128)S(1)} %pad_maximum_fusion.1), channel_id=1, source_target_pairs={{0,256},{64,320},{128,384},{192,448},{256,0},{320,64},{384,128},{4... | collective-permute-start | bytes 2359304 | tf_op jit(solution)/shard_map/ppermute | solution.py:12
  196.0 19.6 %collective-permute-start.2 = (f32[128,2,2,3,128]{0,4,1,3,2:T(8,128)S(1)}, f32[128,2,2,3,128]{0,4,1,3,2:T(8,128)S(1)}, u32[]{:S(2)}, u32[]{:S(2)}) collective-permute-start(f32[128,2,2,3,128]{0,4,1,3,2:T(8,128)S(1)} %pad_maximum_fusion.2), channel_id=1, source_target_pairs={{0,128},{64,192},{128,0},{192,64},{256,384},{320,448},{384,256},{4... | collective-permute-start | bytes 2359304 | tf_op jit(solution)/shard_map/ppermute | solution.py:12
  215.8 6.1 %collective-permute-start.3 = (f32[128,2,2,3,128]{0,4,1,3,2:T(8,128)S(1)}, f32[128,2,2,3,128]{0,4,1,3,2:T(8,128)S(1)}, u32[]{:S(2)}, u32[]{:S(2)}) collective-permute-start(f32[128,2,2,3,128]{0,4,1,3,2:T(8,128)S(1)} %pad_maximum_fusion.3), channel_id=1, source_target_pairs={{0,64},{64,0},{128,192},{192,128},{256,320},{320,256},{384,448},{4... | collective-permute-start | bytes 2359304 | tf_op jit(solution)/shard_map/ppermute | solution.py:12
  224.2 4.2 %collective-permute-start.4 = (f32[128,2,2,3,128]{0,4,3,2,1:T(8,128)S(1)}, f32[128,2,2,3,128]{0,4,3,2,1:T(8,128)S(1)}, u32[]{:S(2)}, u32[]{:S(2)}) collective-permute-start(f32[128,2,2,3,128]{0,4,3,2,1:T(8,128)S(1)} %multiply_bitcast_fusion), channel_id=1, source_target_pairs={{0,64},{64,0},{128,192},{192,128},{256,320},{320,256},{384,448},{4... | collective-permute-start | bytes 2359304 | tf_op jit(solution)/shard_map/ppermute | solution.py:12
  228.8 20.6 %collective-permute-start.5 = (f32[128,2,2,3,128]{0,4,3,2,1:T(8,128)S(1)}, f32[128,2,2,3,128]{0,4,3,2,1:T(8,128)S(1)}, u32[]{:S(2)}, u32[]{:S(2)}) collective-permute-start(f32[128,2,2,3,128]{0,4,3,2,1:T(8,128)S(1)} %get-tuple-element.13), channel_id=1, source_target_pairs={{0,128},{64,192},{128,0},{192,64},{256,384},{320,448},{384,256},{4... | collective-permute-start | bytes 2359304 | tf_op jit(solution)/shard_map/ppermute | solution.py:12
  249.8 38.8 %collective-permute-start.6 = (f32[128,2,2,3,128]{0,4,3,2,1:T(8,128)S(1)}, f32[128,2,2,3,128]{0,4,3,2,1:T(8,128)S(1)}, u32[]{:S(2)}, u32[]{:S(2)}) collective-permute-start(f32[128,2,2,3,128]{0,4,3,2,1:T(8,128)S(1)} %get-tuple-element.11), channel_id=1, source_target_pairs={{0,256},{64,320},{128,384},{192,448},{256,0},{320,64},{384,128},{4... | collective-permute-start | bytes 2359304 | tf_op jit(solution)/shard_map/ppermute | solution.py:12
  289.1 41.0 %collective-permute-start.7 = (f32[128,2,2,3,128]{0,4,3,2,1:T(8,128)S(1)}, f32[128,2,2,3,128]{0,4,3,2,1:T(8,128)S(1)}, u32[]{:S(2)}, u32[]{:S(2)}) collective-permute-start(f32[128,2,2,3,128]{0,4,3,2,1:T(8,128)S(1)} %get-tuple-element.9), channel_id=1, source_target_pairs={{0,512},{64,576},{128,640},{192,704},{256,768},{320,832},{384,896}... | collective-permute-start | bytes 2359304 | tf_op jit(solution)/shard_map/ppermute | solution.py:12
Sparse Core Ops, SparseCore 0:
  12.2 98.9 all-gather.1
where the time goes:
time: 340 us
  waiting for transfers between devices  263 us (77%)
  starting transfers between devices  37.5 us (11%)
  between operations  16 us (5%)
  local copies, waits for them, and re-layouts  11.3 us (3%)
  matrix products  7.15 us (2%)
  other arithmetic  4.12 us (1%)
    ppermute x8, waiting for transfers between devices, from_partner(): return lax.ppermute(value, axis, pairs)  169 us
    all_gather x1, waiting for transfers between devices, per_device(): gathered = lax.all_gather(tokens, 'chan', axis=1, tiled=True)  94.1 us
    ppermute x8, starting transfers between devices, from_partner(): return lax.ppermute(value, axis, pairs)  37.5 us
    unnamed x10, local copies, waits for them, and re-layouts  11.2 us
  transfers between devices with their start and end apart: 9, of which 9 were waited for; matrix products, arithmetic and copies ran while one was open for 3% of the time, Pallas kernels for 0%

commit v1 on v0

v1 whole, which is shorter than its diff:
```python
import functools
import math

import jax
import jax.numpy as jnp
import ml_dtypes
import numpy as np
from jax import lax
from jax.experimental import pallas as pl
from jax.experimental.pallas import tpu as pltpu
from jax.sharding import PartitionSpec as P

MESH = pl.DeviceIdType.MESH
SUBS = 2


def grid_of(chans):
    columns = 1
    while columns * columns < chans:
        columns *= 2
    return chans // columns, columns


def split_table(table):
    high = table.astype(ml_dtypes.bfloat16)
    low = (table - high.astype(np.float64)).astype(ml_dtypes.bfloat16)
    return high, low


def tables(rows):
    angle = math.pi * np.outer(np.arange(2 * rows), 2 * np.arange(rows) + 1) / (2 * rows)
    forward = np.concatenate([np.cos(angle), -np.sin(angle)], axis=1)[:rows]
    inverse = np.concatenate([np.cos(angle), -np.sin(angle)], axis=1).T / rows
    return np.concatenate(split_table(forward), axis=0), np.stack(split_table(inverse))


def dot(left, right):
    return jnp.dot(left, right, preferred_element_type=jnp.float32)


def split(value):
    high = value.astype(jnp.bfloat16)
    return high, (value - high.astype(jnp.float32)).astype(jnp.bfloat16)


def body(
    ny, nz, nseq,
    tok_hbm, w_hbm, filt_hbm, gout_hbm, fwd_hbm, inv_hbm,
    gated, gproj, gfilt,
    tok, filt, gout, w, fwd, inv, abuf, bbuf, acc,
    fsend, frecv, fspec, xsend, xrecv, xspec, prod, ysend, yrecv,
    local_sem, p1_send, p1_recv, ring_send, ring_recv, f_send, f_recv, x_send, x_recv, y_send, y_recv,
):
    rows, width = filt.shape
    half = rows // 2
    per = width // nseq
    seq = lax.axis_index("seq")
    chan = lax.axis_index("chan")
    y, z = chan // nz, chan % nz

    weights = [
        pltpu.make_async_copy(w_hbm.at[b], w.at[:, pl.ds(b * width, width)], local_sem.at[b])
        for b in range(3)
    ]
    constants = [
        pltpu.make_async_copy(fwd_hbm, fwd, local_sem.at[3]),
        pltpu.make_async_copy(inv_hbm, inv, local_sem.at[4]),
    ]
    inputs = [
        pltpu.make_async_copy(tok_hbm, tok, local_sem.at[5]),
        pltpu.make_async_copy(filt_hbm, filt, local_sem.at[6]),
        pltpu.make_async_copy(gout_hbm, gout, local_sem.at[7]),
    ]
    for copy in inputs + constants + weights:
        copy.start()

    barrier = pltpu.get_barrier_semaphore()

    def seq_peer(step):
        return (lax.rem(seq + step, nseq), chan)

    def z_peer(step):
        return (seq, y * nz + lax.rem(z + step, nz))

    def y_peer(step):
        return (seq, lax.rem(y + step, ny) * nz + z)

    for peer, count in ((z_peer, nz), (y_peer, ny), (seq_peer, nseq)):
        def greet(step, carry, peer=peer):
            pl.semaphore_signal(barrier, inc=1, device_id=peer(step), device_id_type=MESH)
            return carry
        lax.fori_loop(1, count, greet, 0)

    for copy in inputs:
        copy.wait()
    abuf[y, z] = tok[:half]
    bbuf[z, y] = tok[half:]
    fsend[...] = filt[...].T.reshape(nseq, per, rows)
    pl.semaphore_wait(barrier, nz + ny + nseq - 3)

    def first(which, step):
        source = tok.at[pl.ds(which * half, half)]
        target = abuf.at[y, z] if which == 0 else bbuf.at[z, y]
        return pltpu.make_async_remote_copy(
            source, target, p1_send.at[which, step], p1_recv.at[which, step],
            device_id=(z_peer if which == 0 else y_peer)(step), device_id_type=MESH,
        )

    def each(count, action):
        def step_of(step, carry):
            action(step)
            return carry
        lax.fori_loop(1, count, step_of, 0)

    each(nz, lambda step: first(0, step).start())
    each(ny, lambda step: first(1, step).start())

    def exchange(source, target, send, recv, step):
        to = lax.rem(seq + step, nseq)
        return pltpu.make_async_remote_copy(
            source.at[to], target.at[seq], send.at[step], recv.at[step],
            device_id=(to, chan), device_id_type=MESH,
        )

    filters = functools.partial(exchange, fsend, frecv, f_send, f_recv)
    each(nseq, lambda step: filters(step).start())
    frecv[seq] = fsend[seq]

    def ring(direction, step, piece, arriving=False):
        sign = 1 if direction % 2 == 0 else -1
        buffer, place, count, across = (abuf, y, ny, nz) if direction < 2 else (bbuf, z, nz, ny)
        hop = (count + sign) % count
        chunk = lax.rem(place + count - sign * (step - (0 if arriving else 1)), count)
        block = buffer.at[chunk, pl.ds(piece * (across // SUBS), across // SUBS)]
        return pltpu.make_async_remote_copy(
            block, block, ring_send.at[direction, step, piece], ring_recv.at[direction, step, piece],
            device_id=(y_peer if direction < 2 else z_peer)(hop), device_id_type=MESH,
        ), chunk

    def multiply(direction, chunk, piece):
        if direction < 2:
            count = nz // SUBS
            left = jnp.concatenate([abuf[chunk, piece * count + i] for i in range(count)], axis=1)
            right = w[pl.ds(pl.multiple_of((chunk * nz + piece * count) * width, width), count * width)]
            acc[:half] += dot(left, right)
        else:
            count = ny // SUBS
            left = jnp.concatenate([bbuf[chunk, piece * count + i] for i in range(count)], axis=1)
            right = jnp.concatenate(
                [
                    w[pl.ds(pl.multiple_of(((piece * count + i) * nz + chunk) * width, width), width)]
                    for i in range(count)
                ],
                axis=0,
            )
            acc[half:] += dot(left, right)

    def sends(direction, step, piece):
        last = (ny if direction < 2 else nz) // 2
        if step < last:
            return True
        return step == last and (piece < SUBS // 2) == (direction % 2 == 0)

    each(nz, lambda step: first(0, step).wait_recv())
    each(ny, lambda step: first(1, step).wait_recv())
    for piece in range(SUBS):
        for direction in range(4):
            if sends(direction, 1, piece):
                ring(direction, 1, piece)[0].start()

    for copy in weights:
        copy.wait()
    acc[...] = jnp.zeros_like(acc)
    for piece in range(SUBS):
        multiply(0, y, piece)
        multiply(2, z, piece)

    each(nseq, lambda step: filters(step).wait_recv())
    for copy in constants:
        copy.wait()
    high, low = split(frecv[...].reshape(nseq * per, rows))
    fspec[...] = (
        dot(jnp.concatenate([high, high], axis=1), fwd[...]) + dot(low, fwd[:rows])
    ).reshape(nseq, per, 2 * rows)

    for step in range(1, max(ny, nz) // 2 + 1):
        for piece in range(SUBS):
            arrived = []
            for direction in range(4):
                if sends(direction, step, piece):
                    copy, chunk = ring(direction, step, piece, arriving=True)
                    copy.wait_recv()
                    if sends(direction, step + 1, piece):
                        ring(direction, step + 1, piece)[0].start()
                    arrived.append((direction, chunk))
            for direction, chunk in arrived:
                multiply(direction, chunk, piece)

    projection = acc[...].astype(jnp.bfloat16).astype(jnp.float32)
    gate_in, gate_out, values = (projection[:, b * width : (b + 1) * width] for b in range(3))
    grad_dense = gout[...].astype(jnp.float32)
    source = (gate_in * values).T.reshape(nseq, per, rows)
    grad_conv = (grad_dense * gate_out).T.reshape(nseq, per, rows)
    xsend[...] = jnp.concatenate([source, grad_conv], axis=1).astype(jnp.bfloat16)
    signals = functools.partial(exchange, xsend, xrecv, x_send, x_recv)
    each(nseq, lambda step: signals(step).start())
    xrecv[seq] = xsend[seq]
    each(nseq, lambda step: signals(step).wait_recv())

    received = xrecv[...].reshape(nseq * 2 * per, rows)
    xspec[...] = dot(jnp.concatenate([received, received], axis=1), fwd[...]).reshape(
        nseq, 2 * per, 2 * rows
    )

    def spectrum(ref, block, first_row):
        return (
            ref[block, first_row : first_row + per, :rows],
            ref[block, first_row : first_row + per, rows:],
        )

    for out in range(nseq):
        re, im = 0.0, 0.0
        for j in range(out + 1):
            f_re, f_im = spectrum(fspec, j, 0)
            s_re, s_im = spectrum(xspec, out - j, 0)
            re = re + (f_re * s_re - f_im * s_im)
            im = im + (f_re * s_im + f_im * s_re)
        prod[out, :per, :rows] = re
        prod[out, :per, rows:] = im
        re, im, re2, im2 = 0.0, 0.0, 0.0, 0.0
        for j in range(nseq - out):
            g_re, g_im = spectrum(xspec, out + j, per)
            f_re, f_im = spectrum(fspec, j, 0)
            s_re, s_im = spectrum(xspec, j, 0)
            re = re + (f_re * g_re + f_im * g_im)
            im = im + (f_re * g_im - f_im * g_re)
            re2 = re2 + (s_re * g_re + s_im * g_im)
            im2 = im2 + (s_re * g_im - s_im * g_re)
        prod[out, per : 2 * per, :rows] = re
        prod[out, per : 2 * per, rows:] = im
        prod[out, 2 * per :, :rows] = re2
        prod[out, 2 * per :, rows:] = im2

    high, low = split(prod[...].reshape(nseq * 3 * per, 2 * rows))
    prod[...] = (dot(high, inv[0]) + dot(low, inv[0]) + dot(high, inv[1])).reshape(
        nseq, 3 * per, 2 * rows
    )
    for block in range(nseq):
        conv = prod[block, :per, :rows]
        grads = prod[block, per:, :rows]
        if block > 0:
            conv = conv + prod[block - 1, :per, rows:]
        if block < nseq - 1:
            grads = grads - prod[block + 1, per:, rows:]
        of_filter = grads[per:]
        rest = of_filter - of_filter.astype(jnp.bfloat16).astype(jnp.float32)
        ysend[block] = jnp.concatenate([conv, grads, rest], axis=0).astype(jnp.bfloat16)
    results = functools.partial(exchange, ysend, yrecv, y_send, y_recv)
    each(nseq, lambda step: results(step).start())
    yrecv[seq] = ysend[seq]
    each(nseq, lambda step: results(step).wait_recv())

    back = yrecv[...].astype(jnp.float32)
    conv_out = back[:, :per].reshape(width, rows).T
    grad_source = back[:, per : 2 * per].reshape(width, rows).T
    of_filter = (back[:, 2 * per : 3 * per] + back[:, 3 * per :]).reshape(width, rows).T
    gated[...] = (gate_out * conv_out).astype(jnp.bfloat16)
    gproj[0] = (grad_source * values).astype(jnp.bfloat16)
    gproj[1] = (grad_dense * conv_out).astype(jnp.bfloat16)
    gproj[2] = (grad_source * gate_in).astype(jnp.bfloat16)
    gfilt[...] = of_filter

    each(nz, lambda step: first(0, step).wait_send())
    each(ny, lambda step: first(1, step).wait_send())
    for step in range(1, max(ny, nz) // 2 + 1):
        for piece in range(SUBS):
            for direction in range(4):
                if sends(direction, step, piece):
                    ring(direction, step, piece)[0].wait_send()
    each(nseq, lambda step: filters(step).wait_send())
    each(nseq, lambda step: signals(step).wait_send())
    each(nseq, lambda step: results(step).wait_send())


def per_device(tokens, in_weight, long_filter, grad_out):
    rows, width = long_filter.shape
    depth = in_weight.shape[0]
    nseq = lax.axis_size("seq")
    ny, nz = grid_of(lax.axis_size("chan"))
    per = width // nseq
    forward, inverse = tables(rows)
    vmem = pl.BlockSpec(memory_space=pltpu.VMEM)
    hbm = pl.BlockSpec(memory_space=pltpu.HBM)
    bf16, f32 = jnp.bfloat16, jnp.float32
    dma = pltpu.SemaphoreType.DMA
    steps = max(ny, nz) // 2 + 1
    gated_out, grad_proj, grad_filter = pl.pallas_call(
        functools.partial(body, ny, nz, nseq),
        name="gather_project_convolve",
        out_shape=(
            jax.ShapeDtypeStruct((rows, width), bf16),
            jax.ShapeDtypeStruct((3, rows, width), bf16),
            jax.ShapeDtypeStruct((rows, width), f32),
        ),
        in_specs=[hbm] * 6,
        out_specs=(vmem, vmem, vmem),
        scratch_shapes=[
            pltpu.VMEM((rows, width), bf16),
            pltpu.VMEM((rows, width), f32),
            pltpu.VMEM((rows, width), bf16),
            pltpu.VMEM((depth, 3 * width), bf16),
            pltpu.VMEM(forward.shape, bf16),
            pltpu.VMEM(inverse.shape, bf16),
            pltpu.VMEM((ny, nz, rows // 2, width), bf16),
            pltpu.VMEM((nz, ny, rows // 2, width), bf16),
            pltpu.VMEM((rows, 3 * width), f32),
            pltpu.VMEM((nseq, per, rows), f32),
            pltpu.VMEM((nseq, per, rows), f32),
            pltpu.VMEM((nseq, per, 2 * rows), f32),
            pltpu.VMEM((nseq, 2 * per, rows), bf16),
            pltpu.VMEM((nseq, 2 * per, rows), bf16),
            pltpu.VMEM((nseq, 2 * per, 2 * rows), f32),
            pltpu.VMEM((nseq, 3 * per, 2 * rows), f32),
            pltpu.VMEM((nseq, 4 * per, rows), bf16),
            pltpu.VMEM((nseq, 4 * per, rows), bf16),
            dma((8,)),
            dma((2, max(ny, nz))),
            dma((2, max(ny, nz))),
            dma((4, steps, SUBS)),
            dma((4, steps, SUBS)),
            dma((nseq,)),
            dma((nseq,)),
            dma((nseq,)),
            dma((nseq,)),
            dma((nseq,)),
            dma((nseq,)),
        ],
        compiler_params=pltpu.CompilerParams(
            collective_id=0, has_side_effects=True, vmem_limit_bytes=56 * 2**20
        ),
    )(
        tokens,
        jnp.transpose(in_weight, (1, 0, 2)),
        long_filter,
        grad_out,
        jnp.asarray(forward),
        jnp.asarray(inverse),
    )
    return gated_out, jnp.transpose(grad_proj, (1, 0, 2)), grad_filter


def solution(mesh):
    in_specs = (P("seq", "chan"), P(None, None, "chan"), P("seq", "chan"), P("seq", "chan"))
    out_specs = (P("seq", "chan"), P("seq", None, "chan"), P("seq", "chan"))
    return jax.shard_map(
        per_device, mesh=mesh, in_specs=in_specs, out_specs=out_specs, check_vma=False
    )
```

time: 340 us -> 66.8 us (0.20)
  waiting for transfers between devices: 263 us -> 0 us
  Pallas kernels: 0 us -> 61.5 us
  starting transfers between devices: 37.5 us -> 0 us
  between operations: 16 us -> 0.64 us
  matrix products: 7.15 us -> 0 us
  local copies, waits for them, and re-layouts: 11.3 us -> 4.39 us
  other arithmetic: 4.12 us -> 0 us
    ppermute x8 -> x0, waiting for transfers between devices: 169 us -> none  [from_partner(): return lax.ppermute(value, axis, pairs)]
    all_gather x1 -> x0, waiting for transfers between devices: 94.1 us -> none  [per_device(): gathered = lax.all_gather(tokens, 'chan', axis=1, tiled=True)]
    pallas_call x0 -> x1, Pallas kernels: none -> 61.5 us  [per_device(): pl.pallas_call(functools.partial(body, ny, nz, nseq), name='gather_projec...]
    ppermute x8 -> x0, starting transfers between devices: 37.5 us -> none  [from_partner(): return lax.ppermute(value, axis, pairs)]
    dot_general x3 -> x0, matrix products: 7.15 us -> none  [the longest x1 5.4 us: per_device(): projected = jnp.dot(gathered, w_flat, preferred_element_type=jnp.float32)]
    unnamed x10 -> x3, local copies, waits for them, and re-layouts: 11.2 us -> 4.39 us
  transfers between devices with their start and end apart: 9 -> 0, of which waited for: 9 -> 0; matrix products, arithmetic and copies ran while one was open for 3% -> 0% of each run, Pallas kernels for 0% -> 0%
where the time goes in v1:
time: 66.8 us; the launch traced here: 66.5 us
  Pallas kernels  61.5 us (92%)
  local copies, waits for them, and re-layouts  4.39 us (7%)
    pallas_call x1, Pallas kernels, per_device(): pl.pallas_call(functools.partial(body, ny, nz, nseq), name='gather_projec...  61.5 us
    unnamed x3, local copies, waits for them, and re-layouts  4.39 us

profile of v1, /device:TPU:1, one launch (start us, length us, event | category | flops | bytes accessed | tf_op | source)
XLA Modules:
  0.0 66.5 jit_solution(14027091309780570929)
XLA Ops:
  0.6 61.5 %gather_project_convolve.1 = (bf16[128,128]{1,0:T(8,128)(2,1)}, bf16[3,128,128]{2,1,0:T(8,128)(2,1)}, f32[128,128]{1,0:T(8,128)}) custom-call(bf16[128,128]{1,0:T(8,128)(2,1)} %tok_hbm.1, bf16[3,8192,128]{2,1,0:T(8,128)(2,1)} %bitcast.2, f32[128,128]{1,0:T(8,128)} %filt_hbm.1, bf16[128,128]{1,0:T(8,128)(2,1)} %gout_hbm.1, ...), custom_call_target="tpu_custom_call" | custom-call | tf_op jit(solution)/shard_map/gather_project_convolve/pallas_call | solution.py:297
  62.2 1.4 %copy.12 = bf16[128,128]{1,0:T(8,128)(2,1)} copy(bf16[128,128]{1,0:T(8,128)(2,1)} %get-tuple-element.12) | data formatting | bytes 65536
  63.5 1.5 %copy.13 = bf16[128,3,128]{2,0,1:T(8,128)(2,1)} copy(bf16[128,3,128]{2,0,1:T(8,128)(2,1)} %bitcast.3) | data formatting | bytes 196608
  65.1 1.5 %copy.14 = f32[128,128]{1,0:T(8,128)} copy(f32[128,128]{1,0:T(8,128)} %get-tuple-element.14) | data formatting | bytes 131072

commit v2 on v1

v2 whole, which is shorter than its diff:
```python
import functools
import math

import jax
import jax.numpy as jnp
import ml_dtypes
import numpy as np
from jax import lax
from jax.experimental import pallas as pl
from jax.experimental.pallas import tpu as pltpu
from jax.sharding import PartitionSpec as P

MESH = pl.DeviceIdType.MESH


def grid_of(chans):
    columns = 1
    while columns * columns < chans:
        columns *= 2
    return chans // columns, columns


def split_table(table):
    high = table.astype(ml_dtypes.bfloat16)
    low = (table - high.astype(np.float64)).astype(ml_dtypes.bfloat16)
    return high, low


def tables(rows):
    angle = math.pi * np.outer(np.arange(2 * rows), 2 * np.arange(rows) + 1) / (2 * rows)
    forward = np.concatenate([np.cos(angle), -np.sin(angle)], axis=1)[:rows]
    inverse = np.concatenate([np.cos(angle), -np.sin(angle)], axis=1).T / rows
    return np.concatenate(split_table(forward), axis=0), np.stack(split_table(inverse))


def dot(left, right):
    return jnp.dot(left, right, preferred_element_type=jnp.float32)


def split(value):
    high = value.astype(jnp.bfloat16)
    return high, (value - high.astype(jnp.float32)).astype(jnp.bfloat16)


def body(
    ny, nz, nseq,
    tok_hbm, w_hbm, filt_hbm, gout_hbm, fwd_hbm, inv_hbm,
    gated, gproj, gfilt,
    filt, gout, w, fwd, inv, tokens, acc,
    fsend, frecv, fspec, xsend, xrecv, xspec, prod, ysend, yrecv,
    local_sem, z_send, z_recv, ring_send, ring_recv, f_send, f_recv, x_send, x_recv, y_send, y_recv,
):
    rows, width = filt.shape
    half = rows // 2
    per = width // nseq
    seq = lax.axis_index("seq")
    chan = lax.axis_index("chan")
    y, z = chan // nz, chan % nz

    weights = [
        pltpu.make_async_copy(w_hbm.at[b], w.at[:, pl.ds(b * width, width)], local_sem.at[b])
        for b in range(3)
    ]
    constants = [
        pltpu.make_async_copy(fwd_hbm, fwd, local_sem.at[3]),
        pltpu.make_async_copy(inv_hbm, inv, local_sem.at[4]),
    ]
    inputs = [
        pltpu.make_async_copy(tok_hbm, tokens.at[z, y], local_sem.at[5]),
        pltpu.make_async_copy(filt_hbm, filt, local_sem.at[6]),
        pltpu.make_async_copy(gout_hbm, gout, local_sem.at[7]),
    ]
    for copy in inputs + constants + weights:
        copy.start()

    barrier = pltpu.get_barrier_semaphore()
    up, down = (seq, lax.rem(y + 1, ny) * nz + z), (seq, lax.rem(y + ny - 1, ny) * nz + z)

    def greet(peer):
        pl.semaphore_signal(barrier, inc=1, device_id=peer, device_id_type=MESH)

    def each(first, last, action):
        def step_of(step, carry):
            action(step)
            return carry
        lax.fori_loop(first, last, step_of, 0)

    greet(up)
    greet(down)
    each(z + 1, nz, lambda other: greet((seq, y * nz + other)))

    @pl.when(seq != 0)
    def _():
        each(1, nseq, lambda step: greet((lax.rem(seq + step, nseq), chan)))

    for copy in inputs:
        copy.wait()
    fsend[...] = filt[...].T.reshape(nseq, per, rows)
    frecv[seq] = fsend[seq]
    acc[...] = jnp.zeros_like(acc)
    pl.semaphore_wait(barrier, 2 + z + jnp.where(seq == 0, nseq - 1, nseq - 2))

    def along_z(other):
        return pltpu.make_async_remote_copy(
            tokens.at[z, y], tokens.at[z, y], z_send.at[other], z_recv.at[z],
            device_id=(seq, y * nz + other), device_id_type=MESH,
        )

    def from_z(other):
        return pltpu.make_async_remote_copy(
            tokens.at[other, y], tokens.at[other, y], z_send.at[other], z_recv.at[other],
            device_id=(seq, y * nz + other), device_id_type=MESH,
        )

    def column(place):
        if place == 0:
            return z
        later = jnp.where(place < z, place, place + 1)
        return jnp.where(z == 0, place, 0 if place == nz - 1 else later)

    columns = [column(place) for place in range(nz)]

    last = ny // 2
    rows_up = [lax.rem(y + ny - step, ny) for step in range(last + 1)]
    rows_down = [lax.rem(y + step, ny) for step in range(last + 1)]

    def ring(way, place, step, arriving=False):
        chunk = (rows_up, rows_down)[way][step if arriving else step - 1]
        block = tokens.at[columns[place], chunk]
        if step == last:
            block = block.at[pl.ds(way * half, half)]
        return pltpu.make_async_remote_copy(
            block, block, ring_send.at[way, place, step], ring_recv.at[way, place, step],
            device_id=(up, down)[way], device_id_type=MESH,
        )

    def multiply(place, chunks):
        left = [tokens[columns[place], chunk] for chunk in chunks]
        right = [
            w[pl.ds(pl.multiple_of((chunk * nz + columns[place]) * width, width), width)]
            for chunk in chunks
        ]
        acc[...] += dot(jnp.concatenate(left, axis=1), jnp.concatenate(right, axis=0))

    def exchange(source, target, send, recv, step):
        to = lax.rem(seq + step, nseq)
        return pltpu.make_async_remote_copy(
            source.at[to], target.at[seq], send.at[step], recv.at[step],
            device_id=(to, chan), device_id_type=MESH,
        )

    others = sorted(range(1, nseq), key=lambda step: abs(step - nseq // 2))
    filters = functools.partial(exchange, fsend, frecv, f_send, f_recv)
    signals = functools.partial(exchange, xsend, xrecv, x_send, x_recv)
    results = functools.partial(exchange, ysend, yrecv, y_send, y_recv)

    each(0, z, lambda other: along_z(other).start())

    def first_filters(step):
        @pl.when(lax.rem(seq + step, nseq) != 0)
        def _():
            filters(step).start()

    def other_filters(step):
        @pl.when(step != seq)
        def _():
            filters(step).wait_recv()

    events = sorted(
        ((place, step) for place in range(nz) for step in range(last + 1)),
        key=lambda event: (event[0] + event[1], event[0]),
    )
    for place, step in events:
        if step == 0 and place > 0:
            from_z(columns[place]).wait_recv()

            @pl.when(columns[place] > z)
            def _(place=place):
                along_z(columns[place]).start()

        if step > 0:
            ring(0, place, step, arriving=True).wait_recv()
            ring(1, place, step, arriving=True).wait_recv()
        if step < last:
            ring(0, place, step + 1).start()
            ring(1, place, step + 1).start()
        if (place, step) == (0, 0):
            each(1, nseq, first_filters)
            for copy in weights:
                copy.wait()
        if step in (0, last):
            multiply(place, [rows_up[step]])
        else:
            multiply(place, [rows_up[step], rows_down[step]])
        if (place, step) == (nz - 1, 0):
            @pl.when(seq != 0)
            def _():
                filters(seq).wait_recv()
                filters(nseq - seq).start()
        if (place, step) == (nz - 1, last - 1):
            each(1, nseq, other_filters)

            for copy in constants:
                copy.wait()
            high, low = split(frecv[...].reshape(nseq * per, rows))
            fspec[...] = (
                dot(jnp.concatenate([high, high], axis=1), fwd[...]) + dot(low, fwd[:rows])
            ).reshape(nseq, per, 2 * rows)

    projection = acc[...].astype(jnp.bfloat16).astype(jnp.float32)
    gate_in, gate_out, values = (projection[:, b * width : (b + 1) * width] for b in range(3))
    grad_dense = gout[...].astype(jnp.float32)
    source = (gate_in * values).T.reshape(nseq, per, rows)
    grad_conv = (grad_dense * gate_out).T.reshape(nseq, per, rows)
    xsend[...] = jnp.concatenate([source, grad_conv], axis=1).astype(jnp.bfloat16)
    for step in others:
        signals(step).start()
    xrecv[seq] = xsend[seq]
    for step in others:
        signals(step).wait_recv()

    received = xrecv[...].reshape(nseq * 2 * per, rows)
    xspec[...] = dot(jnp.concatenate([received, received], axis=1), fwd[...]).reshape(
        nseq, 2 * per, 2 * rows
    )

    def spectrum(ref, block, first_row):
        return (
            ref[block, first_row : first_row + per, :rows],
            ref[block, first_row : first_row + per, rows:],
        )

    for out in range(nseq):
        re, im = 0.0, 0.0
        for j in range(out + 1):
            f_re, f_im = spectrum(fspec, j, 0)
            s_re, s_im = spectrum(xspec, out - j, 0)
            re = re + (f_re * s_re - f_im * s_im)
            im = im + (f_re * s_im + f_im * s_re)
        prod[out, :per, :rows] = re
        prod[out, :per, rows:] = im
        re, im, re2, im2 = 0.0, 0.0, 0.0, 0.0
        for j in range(nseq - out):
            g_re, g_im = spectrum(xspec, out + j, per)
            f_re, f_im = spectrum(fspec, j, 0)
            s_re, s_im = spectrum(xspec, j, 0)
            re = re + (f_re * g_re + f_im * g_im)
            im = im + (f_re * g_im - f_im * g_re)
            re2 = re2 + (s_re * g_re + s_im * g_im)
            im2 = im2 + (s_re * g_im - s_im * g_re)
        prod[out, per : 2 * per, :rows] = re
        prod[out, per : 2 * per, rows:] = im
        prod[out, 2 * per :, :rows] = re2
        prod[out, 2 * per :, rows:] = im2

    high, low = split(prod[...].reshape(nseq * 3 * per, 2 * rows))
    prod[...] = (dot(high, inv[0]) + dot(low, inv[0]) + dot(high, inv[1])).reshape(
        nseq, 3 * per, 2 * rows
    )
    for block in range(nseq):
        conv = prod[block, :per, :rows]
        grads = prod[block, per:, :rows]
        if block > 0:
            conv = conv + prod[block - 1, :per, rows:]
        if block < nseq - 1:
            grads = grads - prod[block + 1, per:, rows:]
        ysend[block] = jnp.concatenate([conv, grads], axis=0).astype(jnp.bfloat16)
    for step in others:
        results(step).start()
    yrecv[seq] = ysend[seq]
    for step in others:
        results(step).wait_recv()

    back = yrecv[...].astype(jnp.float32)
    conv_out = back[:, :per].reshape(width, rows).T
    grad_source = back[:, per : 2 * per].reshape(width, rows).T
    of_filter = back[:, 2 * per :].reshape(width, rows).T
    gated[...] = (gate_out * conv_out).astype(jnp.bfloat16)
    gproj[0] = (grad_source * values).astype(jnp.bfloat16)
    gproj[1] = (grad_dense * conv_out).astype(jnp.bfloat16)
    gproj[2] = (grad_source * gate_in).astype(jnp.bfloat16)
    gfilt[...] = of_filter

    each(0, z, lambda other: along_z(other).wait_send())
    each(z + 1, nz, lambda other: along_z(other).wait_send())
    for place, step in events:
        if step:
            ring(0, place, step).wait_send()
            ring(1, place, step).wait_send()
    for kind in (filters, signals, results):
        for step in others:
            kind(step).wait_send()


def per_device(tokens, in_weight, long_filter, grad_out):
    rows, width = long_filter.shape
    depth = in_weight.shape[0]
    nseq = lax.axis_size("seq")
    ny, nz = grid_of(lax.axis_size("chan"))
    per = width // nseq
    forward, inverse = tables(rows)
    vmem = pl.BlockSpec(memory_space=pltpu.VMEM)
    hbm = pl.BlockSpec(memory_space=pltpu.HBM)
    bf16, f32 = jnp.bfloat16, jnp.float32
    dma = pltpu.SemaphoreType.DMA
    gated_out, grad_proj, grad_filter = pl.pallas_call(
        functools.partial(body, ny, nz, nseq),
        name="gather_project_convolve",
        out_shape=(
            jax.ShapeDtypeStruct((rows, width), bf16),
            jax.ShapeDtypeStruct((3, rows, width), bf16),
            jax.ShapeDtypeStruct((rows, width), f32),
        ),
        in_specs=[hbm] * 6,
        out_specs=(vmem, vmem, vmem),
        scratch_shapes=[
            pltpu.VMEM((rows, width), f32),
            pltpu.VMEM((rows, width), bf16),
            pltpu.VMEM((depth, 3 * width), bf16),
            pltpu.VMEM(forward.shape, bf16),
            pltpu.VMEM(inverse.shape, bf16),
            pltpu.VMEM((nz, ny, rows, width), bf16),
            pltpu.VMEM((rows, 3 * width), f32),
            pltpu.VMEM((nseq, per, rows), f32),
            pltpu.VMEM((nseq, per, rows), f32),
            pltpu.VMEM((nseq, per, 2 * rows), f32),
            pltpu.VMEM((nseq, 2 * per, rows), bf16),
            pltpu.VMEM((nseq, 2 * per, rows), bf16),
            pltpu.VMEM((nseq, 2 * per, 2 * rows), f32),
            pltpu.VMEM((nseq, 3 * per, 2 * rows), f32),
            pltpu.VMEM((nseq, 3 * per, rows), bf16),
            pltpu.VMEM((nseq, 3 * per, rows), bf16),
            dma((8,)),
            dma((nz,)),
            dma((nz,)),
            dma((2, nz, ny // 2 + 1)),
            dma((2, nz, ny // 2 + 1)),
            dma((nseq,)),
            dma((nseq,)),
            dma((nseq,)),
            dma((nseq,)),
            dma((nseq,)),
            dma((nseq,)),
        ],
        compiler_params=pltpu.CompilerParams(
            collective_id=0, has_side_effects=True, vmem_limit_bytes=40 * 2**20
        ),
    )(
        *(
            pltpu.with_memory_space_constraint(operand, pltpu.HBM)
            for operand in (
                tokens,
                jnp.transpose(in_weight, (1, 0, 2)),
                long_filter,
                grad_out,
                jnp.asarray(forward),
                jnp.asarray(inverse),
            )
        )
    )
    return gated_out, jnp.transpose(grad_proj, (1, 0, 2)), grad_filter


def solution(mesh):
    in_specs = (P("seq", "chan"), P(None, None, "chan"), P("seq", "chan"), P("seq", "chan"))
    out_specs = (P("seq", "chan"), P("seq", None, "chan"), P("seq", "chan"))
    return jax.shard_map(
        per_device, mesh=mesh, in_specs=in_specs, out_specs=out_specs, check_vma=False
    )
```

time: 66.8 us -> 85.2 us (1.28)
  the two profiles are of different devices: /device:TPU:1 before, /device:TPU:897 now
where the time goes in v2:
time: 85.2 us; the launch traced here: 85.1 us
  Pallas kernels  82.6 us (97%)
  local copies, waits for them, and re-layouts  1.89 us (2%)
    pallas_call x1, Pallas kernels, per_device(): pl.pallas_call(functools.partial(body, ny, nz, nseq), name='gather_projec...  82.6 us
    unnamed x3, local copies, waits for them, and re-layouts  1.89 us

profile of v2, /device:TPU:897, one launch (start us, length us, event | category | flops | bytes accessed | tf_op | source)
XLA Modules:
  0.0 85.1 jit_solution(18435402934489776541)
XLA Ops:
  0.6 82.6 %gather_project_convolve.1 = (bf16[128,128]{1,0:T(8,128)(2,1)S(1)}, bf16[3,128,128]{2,1,0:T(8,128)(2,1)S(1)}, f32[128,128]{1,0:T(8,128)S(1)}) custom-call(bf16[128,128]{1,0:T(8,128)(2,1)} %tok_hbm.1, bf16[3,8192,128]{2,1,0:T(8,128)(2,1)} %bitcast.3, f32[128,128]{1,0:T(8,128)} %filt_hbm.1, bf16[128,128]{1,0:T(8,128)(2,1)} %gout_hbm.1, ...), custom_call_target="tpu_custom_call" | custom-call | tf_op jit(solution)/shard_map/gather_project_convolve/pallas_call | solution.py:306
  83.2 0.6 copy.12
  83.8 0.6 copy.13
  84.5 0.6 copy.14

commit v3 on v2

--- a/solution.py
+++ b/solution.py
@@ -11,6 +11,20 @@
 from jax.sharding import PartitionSpec as P
 
 MESH = pl.DeviceIdType.MESH
+EARLY = (
+    (0, 0), (0, 1), (1, 0), (0, 2), (2, 0), (1, 1), (0, 3), (2, 1),
+    (3, 0), (1, 2), (0, 4), (2, 2), (3, 1), (1, 3), (4, 0), (5, 0),
+    (6, 0), (7, 0), (3, 2), (2, 3), (4, 1), (1, 4), (5, 1), (6, 1),
+    (7, 1), (3, 3), (2, 4), (4, 2), (5, 2), (6, 2), (7, 2), (3, 4),
+    (4, 3), (5, 3), (6, 3), (7, 3), (4, 4), (5, 4), (6, 4), (7, 4),
+)
+LATE = (
+    (0, 0), (0, 1), (0, 2), (7, 0), (6, 0), (5, 0), (1, 0), (4, 0),
+    (7, 1), (2, 0), (6, 1), (5, 1), (0, 3), (1, 1), (3, 0), (4, 1),
+    (7, 2), (2, 1), (6, 2), (5, 2), (0, 4), (1, 2), (3, 1), (4, 2),
+    (7, 3), (2, 2), (6, 3), (5, 3), (1, 3), (3, 2), (4, 3), (7, 4),
+    (2, 3), (6, 4), (5, 4), (1, 4), (3, 3), (4, 4), (2, 4), (3, 4),
+)
 
 
 def grid_of(chans):
@@ -87,7 +101,20 @@
 
     greet(up)
     greet(down)
-    each(z + 1, nz, lambda other: greet((seq, y * nz + other)))
+
+    def rank(column):
+        return column + jnp.where((column == 0) & (y == 0) & (seq == 0), nz, 0)
+
+    def if_rank(higher, action):
+        def of_other(step):
+            other = lax.rem(z + step, nz)
+
+            @pl.when(rank(other) > rank(z) if higher else rank(other) < rank(z))
+            def _():
+                action(other)
+        each(1, nz, of_other)
+
+    if_rank(True, lambda other: greet((seq, y * nz + other)))
 
     @pl.when(seq != 0)
     def _():
@@ -98,7 +125,8 @@
     fsend[...] = filt[...].T.reshape(nseq, per, rows)
     frecv[seq] = fsend[seq]
     acc[...] = jnp.zeros_like(acc)
-    pl.semaphore_wait(barrier, 2 + z + jnp.where(seq == 0, nseq - 1, nseq - 2))
+    lower = jnp.where((y == 0) & (seq == 0), jnp.where(z == 0, nz - 1, z - 1), z)
+    pl.semaphore_wait(barrier, 2 + lower + jnp.where(seq == 0, nseq - 1, nseq - 2))
 
     def along_z(other):
         return pltpu.make_async_remote_copy(
@@ -154,7 +182,7 @@
     signals = functools.partial(exchange, xsend, xrecv, x_send, x_recv)
     results = functools.partial(exchange, ysend, yrecv, y_send, y_recv)
 
-    each(0, z, lambda other: along_z(other).start())
+    if_rank(False, lambda other: along_z(other).start())
 
     def first_filters(step):
         @pl.when(lax.rem(seq + step, nseq) != 0)
@@ -170,42 +198,45 @@
         ((place, step) for place in range(nz) for step in range(last + 1)),
         key=lambda event: (event[0] + event[1], event[0]),
     )
-    for place, step in events:
-        if step == 0 and place > 0:
-            from_z(columns[place]).wait_recv()
-
-            @pl.when(columns[place] > z)
-            def _(place=place):
-                along_z(columns[place]).start()
-
-        if step > 0:
-            ring(0, place, step, arriving=True).wait_recv()
-            ring(1, place, step, arriving=True).wait_recv()
-        if step < last:
-            ring(0, place, step + 1).start()
-            ring(1, place, step + 1).start()
-        if (place, step) == (0, 0):
-            each(1, nseq, first_filters)
-            for copy in weights:
-                copy.wait()
-        if step in (0, last):
-            multiply(place, [rows_up[step]])
-        else:
-            multiply(place, [rows_up[step], rows_down[step]])
-        if (place, step) == (nz - 1, 0):
-            @pl.when(seq != 0)
-            def _():
-                filters(seq).wait_recv()
-                filters(nseq - seq).start()
-        if (place, step) == (nz - 1, last - 1):
-            each(1, nseq, other_filters)
-
-            for copy in constants:
-                copy.wait()
-            high, low = split(frecv[...].reshape(nseq * per, rows))
-            fspec[...] = (
-                dot(jnp.concatenate([high, high], axis=1), fwd[...]) + dot(low, fwd[:rows])
-            ).reshape(nseq, per, 2 * rows)
+
+    def take(order):
+        for position, (place, step) in enumerate(order):
+            if step == 0 and place > 0:
+                from_z(columns[place]).wait_recv()
+
+                @pl.when(rank(columns[place]) > rank(z))
+                def _(place=place):
+                    along_z(columns[place]).start()
+
+            if step > 0:
+                ring(0, place, step, arriving=True).wait_recv()
+                ring(1, place, step, arriving=True).wait_recv()
+            if step < last:
+                ring(0, place, step + 1).start()
+                ring(1, place, step + 1).start()
+            if position == 0:
+                each(1, nseq, first_filters)
+                for copy in weights:
+                    copy.wait()
+            if step in (0, last):
+                multiply(place, [rows_up[step]])
+            else:
+                multiply(place, [rows_up[step], rows_down[step]])
+            if position == len(order) // 2:
+                @pl.when(seq != 0)
+                def _():
+                    filters(seq).wait_recv()
+                    filters(nseq - seq).start()
+
+    known = (ny, nz) == (8, 8)
+
+    @pl.when(z < nz // 2)
+    def _():
+        take(EARLY if known else events)
+
+    @pl.when(z >= nz // 2)
+    def _():
+        take(LATE if known else events)
 
     projection = acc[...].astype(jnp.bfloat16).astype(jnp.float32)
     gate_in, gate_out, values = (projection[:, b * width : (b + 1) * width] for b in range(3))
@@ -216,6 +247,15 @@
     for step in others:
         signals(step).start()
     xrecv[seq] = xsend[seq]
+
+    each(1, nseq, other_filters)
+    for copy in constants:
+        copy.wait()
+    high, low = split(frecv[...].reshape(nseq * per, rows))
+    fspec[...] = (
+        dot(jnp.concatenate([high, high], axis=1), fwd[...]) + dot(low, fwd[:rows])
+    ).reshape(nseq, per, 2 * rows)
+
     for step in others:
         signals(step).wait_recv()
 

time: 85.2 us -> 75.1 us (0.88)
  the two profiles are of different devices: /device:TPU:897 before, /device:TPU:1 now
where the time goes in v3:
time: 75.1 us; the launch traced here: 74.9 us
  Pallas kernels  72.4 us (96%)
  local copies, waits for them, and re-layouts  1.89 us (3%)
    pallas_call x1, Pallas kernels, per_device(): pl.pallas_call(functools.partial(body, ny, nz, nseq), name='gather_projec...  72.4 us
    unnamed x3, local copies, waits for them, and re-layouts  1.89 us

profile of v3, /device:TPU:1, one launch (start us, length us, event | category | flops | bytes accessed | tf_op | source)
XLA Modules:
  0.0 74.9 jit_solution(2456729424182847773)
XLA Ops:
  0.6 72.4 %gather_project_convolve.1 = (bf16[128,128]{1,0:T(8,128)(2,1)S(1)}, bf16[3,128,128]{2,1,0:T(8,128)(2,1)S(1)}, f32[128,128]{1,0:T(8,128)S(1)}) custom-call(bf16[128,128]{1,0:T(8,128)(2,1)} %tok_hbm.1, bf16[3,8192,128]{2,1,0:T(8,128)(2,1)} %bitcast.3, f32[128,128]{1,0:T(8,128)} %filt_hbm.1, bf16[128,128]{1,0:T(8,128)(2,1)} %gout_hbm.1, ...), custom_call_target="tpu_custom_call" | custom-call | tf_op jit(solution)/shard_map/gather_project_convolve/pallas_call | solution.py:346
  73.0 0.6 copy.12
  73.7 0.6 copy.13
  74.3 0.6 copy.14

commit v4 on v2

--- a/solution.py
+++ b/solution.py
@@ -11,6 +11,12 @@
 from jax.sharding import PartitionSpec as P
 
 MESH = pl.DeviceIdType.MESH
+PIECES = 2
+KEY = 3
+
+
+def by_distance(count):
+    return sorted(range(count), key=lambda offset: (min(offset, count - offset), offset))
 
 
 def grid_of(chans):
@@ -46,9 +52,9 @@
     ny, nz, nseq,
     tok_hbm, w_hbm, filt_hbm, gout_hbm, fwd_hbm, inv_hbm,
     gated, gproj, gfilt,
-    filt, gout, w, fwd, inv, tokens, acc,
+    tok, filt, gout, w, fwd, inv, abuf, bbuf, acc,
     fsend, frecv, fspec, xsend, xrecv, xspec, prod, ysend, yrecv,
-    local_sem, z_send, z_recv, ring_send, ring_recv, f_send, f_recv, x_send, x_recv, y_send, y_recv,
+    local_sem, p1_send, p1_recv, ring_send, ring_recv, f_send, f_recv, x_send, x_recv, y_send, y_recv,
 ):
     rows, width = filt.shape
     half = rows // 2
@@ -66,7 +72,7 @@
         pltpu.make_async_copy(inv_hbm, inv, local_sem.at[4]),
     ]
     inputs = [
-        pltpu.make_async_copy(tok_hbm, tokens.at[z, y], local_sem.at[5]),
+        pltpu.make_async_copy(tok_hbm, tok, local_sem.at[5]),
         pltpu.make_async_copy(filt_hbm, filt, local_sem.at[6]),
         pltpu.make_async_copy(gout_hbm, gout, local_sem.at[7]),
     ]
@@ -74,7 +80,15 @@
         copy.start()
 
     barrier = pltpu.get_barrier_semaphore()
-    up, down = (seq, lax.rem(y + 1, ny) * nz + z), (seq, lax.rem(y + ny - 1, ny) * nz + z)
+
+    def seq_peer(step):
+        return (lax.rem(seq + step, nseq), chan)
+
+    def z_peer(step):
+        return (seq, y * nz + lax.rem(z + step, nz))
+
+    def y_peer(step):
+        return (seq, lax.rem(y + step, ny) * nz + z)
 
     def greet(peer):
         pl.semaphore_signal(barrier, inc=1, device_id=peer, device_id_type=MESH)
@@ -85,62 +99,77 @@
             return carry
         lax.fori_loop(first, last, step_of, 0)
 
-    greet(up)
-    greet(down)
-    each(z + 1, nz, lambda other: greet((seq, y * nz + other)))
+    at_head = (y == 0) & (seq == 0)
+
+    def rank(column):
+        return column + jnp.where((column == 0) & at_head, nz, 0)
+
+    each(1, ny, lambda step: greet(y_peer(step)))
+
+    def greet_higher(step):
+        other = lax.rem(z + step, nz)
+
+        @pl.when(rank(other) > rank(z))
+        def _():
+            greet((seq, y * nz + other))
+
+    each(1, nz, greet_higher)
 
     @pl.when(seq != 0)
     def _():
-        each(1, nseq, lambda step: greet((lax.rem(seq + step, nseq), chan)))
-
-    for copy in inputs:
-        copy.wait()
-    fsend[...] = filt[...].T.reshape(nseq, per, rows)
-    frecv[seq] = fsend[seq]
-    acc[...] = jnp.zeros_like(acc)
-    pl.semaphore_wait(barrier, 2 + z + jnp.where(seq == 0, nseq - 1, nseq - 2))
-
-    def along_z(other):
+        each(1, nseq, lambda step: greet(seq_peer(step)))
+
+    inputs[0].wait()
+    slots_y, slots_z = by_distance(ny), by_distance(nz)
+    abuf[y, 0] = tok[:half]
+    bbuf[z, 0] = tok[half:]
+    lower = jnp.where(at_head, jnp.where(z == 0, nz - 1, z - 1), z)
+    pl.semaphore_wait(barrier, ny - 1 + lower + jnp.where(seq == 0, nseq - 1, nseq - 2))
+
+    def first(which, slot):
+        slots, source = (slots_z, tok.at[pl.ds(0, half)]) if which == 0 else (slots_y, tok.at[pl.ds(half, half)])
+        target = (abuf.at[y] if which == 0 else bbuf.at[z]).at[slot]
         return pltpu.make_async_remote_copy(
-            tokens.at[z, y], tokens.at[z, y], z_send.at[other], z_recv.at[z],
-            device_id=(seq, y * nz + other), device_id_type=MESH,
+            source, target, p1_send.at[which, slot], p1_recv.at[which, slot],
+            device_id=(z_peer if which == 0 else y_peer)(len(slots) - slots[slot]), device_id_type=MESH,
         )
 
-    def from_z(other):
+    steps = [ny // 2, ny // 2, nz // 2, nz // 2]
+    hops = [y_peer(1), y_peer(ny - 1), z_peer(1), z_peer(nz - 1)]
+    chunks = [
+        [
+            lax.rem(place + count - sign * step, count) if step else place
+            for step in range(count // 2 + 1)
+        ]
+        for place, count, sign in ((y, ny, 1), (y, ny, -1), (z, nz, 1), (z, nz, -1))
+    ]
+    size = [(nz if direction < 2 else ny) // PIECES for direction in range(4)]
+
+    def ring(direction, step, piece, arriving=False):
+        buffer = abuf if direction < 2 else bbuf
+        chunk = chunks[direction][step if arriving else step - 1]
+        block = buffer.at[chunk, pl.ds(piece * size[direction], size[direction])]
         return pltpu.make_async_remote_copy(
-            tokens.at[other, y], tokens.at[other, y], z_send.at[other], z_recv.at[other],
-            device_id=(seq, y * nz + other), device_id_type=MESH,
+            block, block, ring_send.at[direction, step, piece], ring_recv.at[direction, step, piece],
+            device_id=hops[direction], device_id_type=MESH,
         )
 
-    def column(place):
-        if place == 0:
-            return z
-        later = jnp.where(place < z, place, place + 1)
-        return jnp.where(z == 0, place, 0 if place == nz - 1 else later)
-
-    columns = [column(place) for place in range(nz)]
-
-    last = ny // 2
-    rows_up = [lax.rem(y + ny - step, ny) for step in range(last + 1)]
-    rows_down = [lax.rem(y + step, ny) for step in range(last + 1)]
-
-    def ring(way, place, step, arriving=False):
-        chunk = (rows_up, rows_down)[way][step if arriving else step - 1]
-        block = tokens.at[columns[place], chunk]
-        if step == last:
-            block = block.at[pl.ds(way * half, half)]
-        return pltpu.make_async_remote_copy(
-            block, block, ring_send.at[way, place, step], ring_recv.at[way, place, step],
-            device_id=(up, down)[way], device_id_type=MESH,
-        )
-
-    def multiply(place, chunks):
-        left = [tokens[columns[place], chunk] for chunk in chunks]
-        right = [
-            w[pl.ds(pl.multiple_of((chunk * nz + columns[place]) * width, width), width)]
-            for chunk in chunks
-        ]
-        acc[...] += dot(jnp.concatenate(left, axis=1), jnp.concatenate(right, axis=0))
+    def sends(direction, step, piece):
+        last = steps[direction]
+        return step < last or (step == last and piece % 2 == direction % 2)
+
+    def multiply(direction, chunk, piece):
+        count, first_slot = size[direction], piece * size[direction]
+        buffer, out = (abuf, pl.ds(0, half)) if direction < 2 else (bbuf, pl.ds(half, half))
+        left = jnp.concatenate([buffer[chunk, first_slot + i] for i in range(count)], axis=1)
+        right = []
+        for i in range(count):
+            if direction < 2:
+                block = chunk * nz + lax.rem(z + slots_z[first_slot + i], nz)
+            else:
+                block = lax.rem(y + slots_y[first_slot + i], ny) * nz + chunk
+            right.append(w[pl.ds(pl.multiple_of(block * width, width), width)])
+        acc[out] += dot(left, jnp.concatenate(right, axis=0))
 
     def exchange(source, target, send, recv, step):
         to = lax.rem(seq + step, nseq)
@@ -154,7 +183,18 @@
     signals = functools.partial(exchange, xsend, xrecv, x_send, x_recv)
     results = functools.partial(exchange, ysend, yrecv, y_send, y_recv)
 
-    each(0, z, lambda other: along_z(other).start())
+    for slot in range(1, max(ny, nz)):
+        for which, count in ((0, nz), (1, ny)):
+            if slot < count and which:
+                first(which, slot).start()
+            elif slot < count:
+                @pl.when(rank(lax.rem(z + nz - slots_z[slot], nz)) < rank(z))
+                def _(slot=slot):
+                    first(0, slot).start()
+
+    for copy in inputs[1:]:
+        copy.wait()
+    fsend[...] = filt[...].T.reshape(nseq, per, rows)
 
     def first_filters(step):
         @pl.when(lax.rem(seq + step, nseq) != 0)
@@ -166,46 +206,47 @@
         def _():
             filters(step).wait_recv()
 
+    each(1, nseq, first_filters)
+    frecv[seq] = fsend[seq]
+    acc[...] = jnp.zeros_like(acc)
+
     events = sorted(
-        ((place, step) for place in range(nz) for step in range(last + 1)),
-        key=lambda event: (event[0] + event[1], event[0]),
+        ((step, piece) for step in range(max(steps) + 1) for piece in range(PIECES)),
+        key=lambda event: (KEY * event[0] + event[1], event[0]),
     )
-    for place, step in events:
-        if step == 0 and place > 0:
-            from_z(columns[place]).wait_recv()
-
-            @pl.when(columns[place] > z)
-            def _(place=place):
-                along_z(columns[place]).start()
-
-        if step > 0:
-            ring(0, place, step, arriving=True).wait_recv()
-            ring(1, place, step, arriving=True).wait_recv()
-        if step < last:
-            ring(0, place, step + 1).start()
-            ring(1, place, step + 1).start()
-        if (place, step) == (0, 0):
-            each(1, nseq, first_filters)
+    ready = False
+    for step, piece in events:
+        arrived = []
+        for direction in range(4):
+            if step == 0:
+                if direction % 2 == 0:
+                    for slot in range(piece * size[direction], (piece + 1) * size[direction]):
+                        if slot:
+                            first(direction // 2, slot).wait_recv()
+                        if slot and direction == 0:
+                            back = slots_z.index(nz - slots_z[slot])
+
+                            @pl.when(rank(lax.rem(z + slots_z[slot], nz)) > rank(z))
+                            def _(back=back):
+                                first(0, back).start()
+
+                    arrived.append(direction)
+            elif sends(direction, step, piece):
+                ring(direction, step, piece, arriving=True).wait_recv()
+                arrived.append(direction)
+            if (step == 0 or direction in arrived) and sends(direction, step + 1, piece):
+                ring(direction, step + 1, piece).start()
+        if not ready:
             for copy in weights:
                 copy.wait()
-        if step in (0, last):
-            multiply(place, [rows_up[step]])
-        else:
-            multiply(place, [rows_up[step], rows_down[step]])
-        if (place, step) == (nz - 1, 0):
-            @pl.when(seq != 0)
-            def _():
-                filters(seq).wait_recv()
-                filters(nseq - seq).start()
-        if (place, step) == (nz - 1, last - 1):
-            each(1, nseq, other_filters)
-
-            for copy in constants:
-                copy.wait()
-            high, low = split(frecv[...].reshape(nseq * per, rows))
-            fspec[...] = (
-                dot(jnp.concatenate([high, high], axis=1), fwd[...]) + dot(low, fwd[:rows])
-            ).reshape(nseq, per, 2 * rows)
+            ready = True
+        for direction in arrived:
+            multiply(direction, chunks[direction][step], piece)
+
+    @pl.when(seq != 0)
+    def _():
+        filters(seq).wait_recv()
+        filters(nseq - seq).start()
 
     projection = acc[...].astype(jnp.bfloat16).astype(jnp.float32)
     gate_in, gate_out, values = (projection[:, b * width : (b + 1) * width] for b in range(3))
@@ -216,6 +257,15 @@
     for step in others:
         signals(step).start()
     xrecv[seq] = xsend[seq]
+
+    each(1, nseq, other_filters)
+    for copy in constants:
+        copy.wait()
+    high, low = split(frecv[...].reshape(nseq * per, rows))
+    fspec[...] = (
+        dot(jnp.concatenate([high, high], axis=1), fwd[...]) + dot(low, fwd[:rows])
+    ).reshape(nseq, per, 2 * rows)
+
     for step in others:
         signals(step).wait_recv()
 
@@ -281,12 +331,13 @@
     gproj[2] = (grad_source * gate_in).astype(jnp.bfloat16)
     gfilt[...] = of_filter
 
-    each(0, z, lambda other: along_z(other).wait_send())
-    each(z + 1, nz, lambda other: along_z(other).wait_send())
-    for place, step in events:
-        if step:
-            ring(0, place, step).wait_send()
-            ring(1, place, step).wait_send()
+    for which, count in ((0, nz), (1, ny)):
+        for slot in range(1, count):
+            first(which, slot).wait_send()
+    for step, piece in events:
+        for direction in range(4):
+            if step and sends(direction, step, piece):
+                ring(direction, step, piece).wait_send()
     for kind in (filters, signals, results):
         for step in others:
             kind(step).wait_send()
@@ -303,6 +354,7 @@
     hbm = pl.BlockSpec(memory_space=pltpu.HBM)
     bf16, f32 = jnp.bfloat16, jnp.float32
     dma = pltpu.SemaphoreType.DMA
+    steps = max(ny, nz) // 2 + 1
     gated_out, grad_proj, grad_filter = pl.pallas_call(
         functools.partial(body, ny, nz, nseq),
         name="gather_project_convolve",
@@ -314,12 +366,14 @@
         in_specs=[hbm] * 6,
         out_specs=(vmem, vmem, vmem),
         scratch_shapes=[
+            pltpu.VMEM((rows, width), bf16),
             pltpu.VMEM((rows, width), f32),
             pltpu.VMEM((rows, width), bf16),
             pltpu.VMEM((depth, 3 * width), bf16),
             pltpu.VMEM(forward.shape, bf16),
             pltpu.VMEM(inverse.shape, bf16),
-            pltpu.VMEM((nz, ny, rows, width), bf16),
+            pltpu.VMEM((ny, nz, rows // 2, width), bf16),
+            pltpu.VMEM((nz, ny, rows // 2, width), bf16),
             pltpu.VMEM((rows, 3 * width), f32),
             pltpu.VMEM((nseq, per, rows), f32),
             pltpu.VMEM((nseq, per, rows), f32),
@@ -331,10 +385,10 @@
             pltpu.VMEM((nseq, 3 * per, rows), bf16),
             pltpu.VMEM((nseq, 3 * per, rows), bf16),
             dma((8,)),
-            dma((nz,)),
-            dma((nz,)),
-            dma((2, nz, ny // 2 + 1)),
-            dma((2, nz, ny // 2 + 1)),
+            dma((2, max(ny, nz))),
+            dma((2, max(ny, nz))),
+            dma((4, steps, PIECES)),
+            dma((4, steps, PIECES)),
             dma((nseq,)),
             dma((nseq,)),
             dma((nseq,)),

time: 85.2 us -> 68.4 us (0.80)
  the two profiles are of different devices: /device:TPU:897 before, /device:TPU:1 now
where the time goes in v4:
time: 68.4 us; the launch traced here: 68.3 us
  Pallas kernels  65.8 us (96%)
  local copies, waits for them, and re-layouts  1.89 us (3%)
    pallas_call x1, Pallas kernels, per_device(): pl.pallas_call(functools.partial(body, ny, nz, nseq), name='gather_projec...  65.8 us
    unnamed x3, local copies, waits for them, and re-layouts  1.89 us

profile of v4, /device:TPU:1, one launch (start us, length us, event | category | flops | bytes accessed | tf_op | source)
XLA Modules:
  0.0 68.3 jit_solution(11354627019814531429)
XLA Ops:
  0.6 65.8 %gather_project_convolve.1 = (bf16[128,128]{1,0:T(8,128)(2,1)S(1)}, bf16[3,128,128]{2,1,0:T(8,128)(2,1)S(1)}, f32[128,128]{1,0:T(8,128)S(1)}) custom-call(bf16[128,128]{1,0:T(8,128)(2,1)} %tok_hbm.1, bf16[3,8192,128]{2,1,0:T(8,128)(2,1)} %bitcast.3, f32[128,128]{1,0:T(8,128)} %filt_hbm.1, bf16[128,128]{1,0:T(8,128)(2,1)} %gout_hbm.1, ...), custom_call_target="tpu_custom_call" | custom-call | tf_op jit(solution)/shard_map/gather_project_convolve/pallas_call | solution.py:358
  66.4 0.6 copy.12
  67.0 0.6 copy.13
  67.7 0.6 copy.14

commit v5 on v4

--- a/solution.py
+++ b/solution.py
@@ -90,41 +90,17 @@
     def y_peer(step):
         return (seq, lax.rem(y + step, ny) * nz + z)
 
-    def greet(peer):
-        pl.semaphore_signal(barrier, inc=1, device_id=peer, device_id_type=MESH)
-
-    def each(first, last, action):
-        def step_of(step, carry):
-            action(step)
+    for peer, count in ((z_peer, nz), (y_peer, ny), (seq_peer, nseq)):
+        def greet(step, carry, peer=peer):
+            pl.semaphore_signal(barrier, inc=1, device_id=peer(step), device_id_type=MESH)
             return carry
-        lax.fori_loop(first, last, step_of, 0)
-
-    at_head = (y == 0) & (seq == 0)
-
-    def rank(column):
-        return column + jnp.where((column == 0) & at_head, nz, 0)
-
-    each(1, ny, lambda step: greet(y_peer(step)))
-
-    def greet_higher(step):
-        other = lax.rem(z + step, nz)
-
-        @pl.when(rank(other) > rank(z))
-        def _():
-            greet((seq, y * nz + other))
-
-    each(1, nz, greet_higher)
-
-    @pl.when(seq != 0)
-    def _():
-        each(1, nseq, lambda step: greet(seq_peer(step)))
+        lax.fori_loop(1, count, greet, 0)
 
     inputs[0].wait()
     slots_y, slots_z = by_distance(ny), by_distance(nz)
     abuf[y, 0] = tok[:half]
     bbuf[z, 0] = tok[half:]
-    lower = jnp.where(at_head, jnp.where(z == 0, nz - 1, z - 1), z)
-    pl.semaphore_wait(barrier, ny - 1 + lower + jnp.where(seq == 0, nseq - 1, nseq - 2))
+    pl.semaphore_wait(barrier, nz + ny + nseq - 3)
 
     def first(which, slot):
         slots, source = (slots_z, tok.at[pl.ds(0, half)]) if which == 0 else (slots_y, tok.at[pl.ds(half, half)])
@@ -185,28 +161,13 @@
 
     for slot in range(1, max(ny, nz)):
         for which, count in ((0, nz), (1, ny)):
-            if slot < count and which:
+            if slot < count:
                 first(which, slot).start()
-            elif slot < count:
-                @pl.when(rank(lax.rem(z + nz - slots_z[slot], nz)) < rank(z))
-                def _(slot=slot):
-                    first(0, slot).start()
-
     for copy in inputs[1:]:
         copy.wait()
     fsend[...] = filt[...].T.reshape(nseq, per, rows)
-
-    def first_filters(step):
-        @pl.when(lax.rem(seq + step, nseq) != 0)
-        def _():
-            filters(step).start()
-
-    def other_filters(step):
-        @pl.when(step != seq)
-        def _():
-            filters(step).wait_recv()
-
-    each(1, nseq, first_filters)
+    for step in others:
+        filters(step).start()
     frecv[seq] = fsend[seq]
     acc[...] = jnp.zeros_like(acc)
 
@@ -223,13 +184,6 @@
                     for slot in range(piece * size[direction], (piece + 1) * size[direction]):
                         if slot:
                             first(direction // 2, slot).wait_recv()
-                        if slot and direction == 0:
-                            back = slots_z.index(nz - slots_z[slot])
-
-                            @pl.when(rank(lax.rem(z + slots_z[slot], nz)) > rank(z))
-                            def _(back=back):
-                                first(0, back).start()
-
                     arrived.append(direction)
             elif sends(direction, step, piece):
                 ring(direction, step, piece, arriving=True).wait_recv()
@@ -243,11 +197,6 @@
         for direction in arrived:
             multiply(direction, chunks[direction][step], piece)
 
-    @pl.when(seq != 0)
-    def _():
-        filters(seq).wait_recv()
-        filters(nseq - seq).start()
-
     projection = acc[...].astype(jnp.bfloat16).astype(jnp.float32)
     gate_in, gate_out, values = (projection[:, b * width : (b + 1) * width] for b in range(3))
     grad_dense = gout[...].astype(jnp.float32)
@@ -258,7 +207,8 @@
         signals(step).start()
     xrecv[seq] = xsend[seq]
 
-    each(1, nseq, other_filters)
+    for step in others:
+        filters(step).wait_recv()
     for copy in constants:
         copy.wait()
     high, low = split(frecv[...].reshape(nseq * per, rows))

time: 68.4 us -> 60.5 us (0.88)
  Pallas kernels: 65.8 us -> 57.9 us
    pallas_call x1, Pallas kernels: 65.8 us -> 57.9 us  [per_device(): pl.pallas_call(functools.partial(body, ny, nz, nseq), name='gather_projec...]
where the time goes in v5:
time: 60.5 us; the launch traced here: 60.4 us
  Pallas kernels  57.9 us (96%)
  local copies, waits for them, and re-layouts  1.89 us (3%)
  between operations  0.64 us (1%)
    pallas_call x1, Pallas kernels, per_device(): pl.pallas_call(functools.partial(body, ny, nz, nseq), name='gather_projec...  57.9 us
    unnamed x3, local copies, waits for them, and re-layouts  1.89 us

profile of v5, /device:TPU:1, one launch (start us, length us, event | category | flops | bytes accessed | tf_op | source)
XLA Modules:
  0.0 60.4 jit_solution(15607175814714746701)
XLA Ops:
  0.6 57.9 %gather_project_convolve.1 = (bf16[128,128]{1,0:T(8,128)(2,1)S(1)}, bf16[3,128,128]{2,1,0:T(8,128)(2,1)S(1)}, f32[128,128]{1,0:T(8,128)S(1)}) custom-call(bf16[128,128]{1,0:T(8,128)(2,1)} %tok_hbm.1, bf16[3,8192,128]{2,1,0:T(8,128)(2,1)} %bitcast.3, f32[128,128]{1,0:T(8,128)} %filt_hbm.1, bf16[128,128]{1,0:T(8,128)(2,1)} %gout_hbm.1, ...), custom_call_target="tpu_custom_call" | custom-call | tf_op jit(solution)/shard_map/gather_project_convolve/pallas_call | solution.py:308
  58.5 0.6 %copy.12 = bf16[128,128]{1,0:T(8,128)(2,1)} copy(bf16[128,128]{1,0:T(8,128)(2,1)S(1)} %get-tuple-element.12) | data formatting | bytes 65536
  59.1 0.6 %copy.13 = bf16[128,3,128]{2,0,1:T(8,128)(2,1)} copy(bf16[128,3,128]{2,0,1:T(8,128)(2,1)S(1)} %bitcast.2) | data formatting | bytes 196608
  59.8 0.6 %copy.14 = f32[128,128]{1,0:T(8,128)} copy(f32[128,128]{1,0:T(8,128)S(1)} %get-tuple-element.14) | data formatting | bytes 131072

commit v6 on v5

--- a/solution.py
+++ b/solution.py
@@ -257,16 +257,15 @@
     prod[...] = (dot(high, inv[0]) + dot(low, inv[0]) + dot(high, inv[1])).reshape(
         nseq, 3 * per, 2 * rows
     )
-    for block in range(nseq):
-        conv = prod[block, :per, :rows]
-        grads = prod[block, per:, :rows]
-        if block > 0:
-            conv = conv + prod[block - 1, :per, rows:]
-        if block < nseq - 1:
-            grads = grads - prod[block + 1, per:, rows:]
+    for step in others + [0]:
+        block = lax.rem(seq + step, nseq)
+        before = prod[jnp.maximum(block - 1, 0), :per, rows:]
+        after = prod[jnp.minimum(block + 1, nseq - 1), per:, rows:]
+        conv = prod[block, :per, :rows] + jnp.where(block > 0, before, 0.0)
+        grads = prod[block, per:, :rows] - jnp.where(block < nseq - 1, after, 0.0)
         ysend[block] = jnp.concatenate([conv, grads], axis=0).astype(jnp.bfloat16)
-    for step in others:
-        results(step).start()
+        if step:
+            results(step).start()
     yrecv[seq] = ysend[seq]
     for step in others:
         results(step).wait_recv()

time: 60.5 us -> 60.5 us (level)
  no operation moved by 1% of the time
where the time goes in v6:
time: 60.5 us; the launch traced here: 60.4 us
  Pallas kernels  57.9 us (96%)
  local copies, waits for them, and re-layouts  1.89 us (3%)
  between operations  0.64 us (1%)
    pallas_call x1, Pallas kernels, per_device(): pl.pallas_call(functools.partial(body, ny, nz, nseq), name='gather_projec...  57.9 us
    unnamed x3, local copies, waits for them, and re-layouts  1.89 us

profile of v6, /device:TPU:1, one launch (start us, length us, event | category | flops | bytes accessed | tf_op | source)
XLA Modules:
  0.0 60.4 jit_solution(8202330049590382702)
XLA Ops:
  0.6 57.9 %gather_project_convolve.1 = (bf16[128,128]{1,0:T(8,128)(2,1)S(1)}, bf16[3,128,128]{2,1,0:T(8,128)(2,1)S(1)}, f32[128,128]{1,0:T(8,128)S(1)}) custom-call(bf16[128,128]{1,0:T(8,128)(2,1)} %tok_hbm.1, bf16[3,8192,128]{2,1,0:T(8,128)(2,1)} %bitcast.3, f32[128,128]{1,0:T(8,128)} %filt_hbm.1, bf16[128,128]{1,0:T(8,128)(2,1)} %gout_hbm.1, ...), custom_call_target="tpu_custom_call" | custom-call | tf_op jit(solution)/shard_map/gather_project_convolve/pallas_call | solution.py:307
  58.5 0.6 %copy.12 = bf16[128,128]{1,0:T(8,128)(2,1)} copy(bf16[128,128]{1,0:T(8,128)(2,1)S(1)} %get-tuple-element.12) | data formatting | bytes 65536
  59.1 0.6 %copy.13 = bf16[128,3,128]{2,0,1:T(8,128)(2,1)} copy(bf16[128,3,128]{2,0,1:T(8,128)(2,1)S(1)} %bitcast.2) | data formatting | bytes 196608
  59.8 0.6 %copy.14 = f32[128,128]{1,0:T(8,128)} copy(f32[128,128]{1,0:T(8,128)S(1)} %get-tuple-element.14) | data formatting | bytes 131072
